TPU v7x, 256 devices: a whole 4x4x8 slice. The times are simulated.
256 devices in a mesh: dp: 16 (over y, x_lo, core), feat: 16 (over x_hi, z).
Axes of the slice: x: 4 (x_hi: 2, x_lo: 2; x = x_hi * 2 + x_lo), y: 4, z: 8, core: 2. Of those that a mesh axis runs over, the one named last changes fastest.
Arguments:
- samples: bfloat16 [12288, 256], P('dp'), may hold values from -6 to 6
- targets: bfloat16 [12288], P('dp'), may hold values from -6 to 6
- counts: int32 [16], replicated, may hold values from 1 to 768, 6144 in all
- bucket_ids: int32 [3, 256], replicated, may hold values from 0 to 4095
- sign_bits: int32 [3, 256], replicated, may hold values from 0 to 1
Outputs:
- gram: float32 [4096, 4096], P('dp', 'feat')
- zty: float32 [4096], P('feat')
Inputs may be any that keep to these rules, and one draw needn't show every extreme that they name: The counts sum to 6144, and some index of dp has exactly 768 live rows.
All inputs are finite; a program needn't handle non-finite values.
Results may differ from a plain program's by a relative error of at most 0.0048.
Values may be sent and summed in bfloat16 or wider, within the bound.
A program may use at most 64 MiB of HBM per device.

v0:
```python
import math

import jax
import jax.numpy as jnp
from jax import lax
from jax.sharding import PartitionSpec as P

DIN = 256
SK = 4096
BAL_DEV = 384


def inverse_terms(spectra_pair, freq_ids, column_ids):
    turns = freq_ids[:, None] * column_ids[None, :] % SK
    angles = turns.astype(jnp.float32) * (2.0 * math.pi / SK)
    cosine = jnp.cos(angles).astype(jnp.bfloat16)
    sine = jnp.sin(angles).astype(jnp.bfloat16)
    first_term = jnp.einsum(
        "fc,rf->cr", cosine, spectra_pair[0], preferred_element_type=jnp.float32
    )
    second_term = jnp.einsum("fc,rf->cr", sine, spectra_pair[1], preferred_element_type=jnp.float32)
    return first_term - second_term


def complex_times(real_a, imag_a, real_b, imag_b):
    return (real_a * real_b - imag_a * imag_b, real_a * imag_b + imag_a * real_b)


def body(samples, targets, counts, bucket_ids, sign_bits):
    device_row = lax.axis_index("dp")
    local_count = counts[device_row]
    live_mask = (jnp.arange(samples.shape[0], dtype=jnp.int32) < local_count).astype(jnp.float32)
    values = samples.astype(jnp.float32)
    normed = (
        values
        * lax.rsqrt(jnp.mean(values * values, axis=-1, keepdims=True) + 1e-06)
        * DIN ** (-0.5)
    )
    normed = normed * live_mask[:, None]
    freq_panel = SK // lax.axis_size("feat")
    own_ids = lax.axis_index("feat") * freq_panel + jnp.arange(freq_panel, dtype=jnp.int32)
    turns = bucket_ids[:, :, None] * own_ids[None, None, :] % SK
    angles = turns.astype(jnp.float32) * (2.0 * math.pi / SK)
    signed = (2 * sign_bits - 1).astype(jnp.float32)[:, :, None]
    table = jnp.stack([signed * jnp.cos(angles), -signed * jnp.sin(angles)], axis=1)
    table = jnp.transpose(table, (2, 0, 1, 3)).reshape(DIN, 6 * freq_panel)
    spectrum_all = jnp.dot(
        normed, table, precision=lax.Precision.HIGHEST, preferred_element_type=jnp.float32
    )
    spectrum_all = spectrum_all.reshape(normed.shape[0], 3, 2, freq_panel)
    real_mix, imag_mix = complex_times(
        spectrum_all[:, 0, 0], spectrum_all[:, 0, 1], spectrum_all[:, 1, 0], spectrum_all[:, 1, 1]
    )
    real_mix, imag_mix = complex_times(
        real_mix, imag_mix, spectrum_all[:, 2, 0], spectrum_all[:, 2, 1]
    )
    spectra_pair = jnp.stack([real_mix.astype(jnp.bfloat16), imag_mix.astype(jnp.bfloat16)], axis=0)
    portion = lax.all_gather(spectra_pair, "feat", axis=2, tiled=True)
    freq_ids = jnp.arange(portion.shape[2], dtype=jnp.int32)
    summed = inverse_terms(portion, freq_ids, own_ids)
    features = (summed * SK ** (-0.5)).astype(jnp.bfloat16)
    partial_gram = lax.dot_general(
        lax.all_gather(features, "feat", axis=0, tiled=True),
        features,
        (((1,), (1,)), ((), ())),
        preferred_element_type=jnp.float32,
    )
    gram_local = lax.psum_scatter(partial_gram, "dp", scatter_dimension=0, tiled=True)
    target_part = lax.dot_general(
        features, targets, (((1,), (0,)), ((), ())), preferred_element_type=jnp.float32
    )
    target_sum = lax.psum(target_part, "dp")
    total_rows = BAL_DEV * lax.axis_size("dp")
    return (gram_local / total_rows, target_sum * total_rows ** (-0.5))


def solution(mesh):
    placed = (P("dp", None), P("dp"), P(), P(), P())
    return jax.shard_map(
        body, mesh=mesh, in_specs=placed, out_specs=(P("dp", "feat"), P("feat")), check_vma=False
    )
```

profile of v0, /device:TPU:1, one launch (start us, length us, event | category | flops | bytes accessed | tf_op | source)
XLA Modules:
  0.0 455.8 jit_solution(16290275978402960558)
XLA Ops:
  7.2 0.0 all-gather.3.cloned.1.call-start
  7.2 0.7 add_convert_fusion.1
  7.9 0.7 fusion.37
  8.6 1.2 fusion.16
  9.8 1.2 dynamic_slice.3
  11.0 0.6 add_rsqrt_fusion
  11.7 3.9 cosine_multiply_fusion
  15.6 5.2 %fusion.10 = f32[768,3,2,256]{3,0,2,1:T(8,128)S(1)} fusion(f32[3,1,256,256]{2,3,1,0:T(8,128)S(1)} %get-tuple-element.6, f32[3,1,256,256]{2,3,1,0:T(8,128)S(1)} %get-tuple-element.5, bf16[768,256]{1,0:T(8,128)(2,1)} %param.5, f32[768]{0:T(1024)S(1)} %get-tuple-element.8, f32[768]{0:T(1024)S(1)} %get-tuple-element.7), kind=kOutput, calls=%fused_computation.16 | convolution fusion | flops 3624861696 | bytes 6690816 | tf_op jit(solution)/shard_map/dot_general | solution.py:47
  20.8 0.3 fusion.23
  21.1 0.2 fusion.24
  21.4 1.0 pad_maximum_fusion
  22.4 0.0 all-gather.3.cloned.1.call-update
  22.4 0.0 all-gather.5.cloned.1.call-start
  22.5 192.8 %all-gather.3.cloned.1.call-done = bf16[2,768,4096]{2,1,0:T(8,128)(2,1)} async-done(((bf16[2,768,256]{2,1,0:T(8,128)(2,1)}), bf16[2,768,4096]{2,1,0:T(8,128)(2,1)}) %all-gather.3.cloned.1.call-update) | async-done | bytes 12582928 | tf_op jit(solution)/shard_map/all_gather | solution.py:58
  215.2 0.0 copy-start.2
  215.2 21.4 %fusion = f32[256,768]{1,0:T(8,128)S(1)} fusion(bf16[2,768,4096]{2,1,0:T(8,128)(2,1)} %all-gather.3.cloned.1.call-done, s32[256]{0:T(256)S(1)} %iota_add_fusion), kind=kOutput, calls=%fused_computation.1 | convolution fusion | flops 1626341376 | bytes 7078912 | tf_op jit(solution)/shard_map/fc,rf->cr/dot_general | solution.py:21
  236.7 0.0 copy-done.2
  236.7 21.1 %fusion.15 = bf16[256,768]{1,0:T(8,128)(2,1)} fusion(f32[256,768]{1,0:T(8,128)S(1)} %fusion, bf16[2,768,4096]{2,1,0:T(8,128)(2,1)S(1)} %copy-done.2, s32[256]{0:T(256)S(1)} %iota_add_fusion), kind=kOutput, calls=%fused_computation.24 | convolution fusion | flops 1626931200 | bytes 7472128 | tf_op jit(solution)/shard_map/fc,rf->cr/dot_general | solution.py:18
  257.8 0.0 all-gather.5.cloned.1.call-update
  257.8 0.0 reduce-scatter.2.cloned.1.call-start
  257.9 113.5 %all-gather.5.cloned.1.call-done = bf16[4096,768]{1,0:T(8,128)(2,1)} async-done(((bf16[256,768]{1,0:T(8,128)(2,1)}), bf16[4096,768]{1,0:T(8,128)(2,1)}) %all-gather.5.cloned.1.call-update) | async-done | bytes 6291472 | tf_op jit(solution)/shard_map/all_gather | solution.py:63
  371.4 6.7 %fusion.38 = f32[4096,256]{1,0:T(8,128)} fusion(bf16[4096,768]{1,0:T(8,128)(2,1)} %all-gather.5.cloned.1.call-done, bf16[256,768]{1,0:T(8,128)(2,1)} %fusion.15), kind=kOutput, calls=%fused_computation.63 | convolution fusion | flops 1610612736 | bytes 10878976 | tf_op jit(solution)/shard_map/dot_general | solution.py:62
  378.0 0.0 copy-start.1
  378.0 0.0 copy-start
  378.0 0.0 reduce-scatter.2.cloned.1.call-update
  378.1 0.7 copy-done.1
  378.7 0.3 copy-done
  379.0 0.2 fusion.39
  379.2 29.1 %psum.7 = f32[256]{0:T(256)S(1)} all-reduce(f32[256]{0:T(256)S(1)} %bitcast.36), channel_id=1, replica_groups=mesh['dp'=16,'feat'=16] {'dp'}, use_global_device_ids=true, to_apply=%region_2.3 | all-reduce | flops 256 | bytes 2048 | tf_op jit(solution)/shard_map/psum | solution.py:72
  408.3 0.6 broadcast_multiply_fusion.1
  408.9 38.7 %reduce-scatter.2.cloned.1.call-done = f32[256,256]{1,0:T(8,128)} async-done(((f32[4096,256]{1,0:T(8,128)}), f32[256,256]{1,0:T(8,128)}) %reduce-scatter.2.cloned.1.call-update) | async-done | bytes 262160 | tf_op jit(solution)/shard_map/reduce_scatter | solution.py:68
  447.6 1.7 broadcast_multiply_fusion
  (2 shorter events, 0.0 us)
Async XLA Ops:
  7.2 208.1 %all-gather.3.cloned.1.call-start = ((), (), s32[]{:S(2)}) async-start(), calls=%async_computation.1 | async-start | bytes 13369344 | tf_op jit(solution)/shard_map/all_gather | solution.py:58
  22.4 349.0 %all-gather.5.cloned.1.call-start = ((), (), s32[]{:S(2)}) async-start(), calls=%async_computation.2 | async-start | bytes 6684672 | tf_op jit(solution)/shard_map/all_gather | solution.py:63
  215.2 21.4 %copy-start.2 = (bf16[2,768,4096]{2,1,0:T(8,128)(2,1)S(1)}, bf16[2,768,4096]{2,1,0:T(8,128)(2,1)}, u32[]{:S(2)}) copy-start(bf16[2,768,4096]{2,1,0:T(8,128)(2,1)} %all-gather.3.cloned.1.call-done) | copy-start | bytes 37748740
  257.8 189.8 %reduce-scatter.2.cloned.1.call-start = ((), (), s32[]{:S(2)}) async-start(), calls=%async_computation.3 | async-start | bytes 4456448 | tf_op jit(solution)/shard_map/reduce_scatter | solution.py:68
  378.0 0.7 copy-start.1
  378.0 1.0 copy-start
Sparse Core Ops, SparseCore 0:
  22.5 192.6 all-gather.2
  258.0 113.3 all-gather.4
  378.2 69.3 reduce-scatter.1
where the time goes:
time: 457 us; the launch traced here: 456 us
  waiting for transfers between devices  345 us (75%)
  matrix products  54.6 us (12%)
  blocking collectives  29.1 us (6%)
  between operations  13.8 us (3%)
  other arithmetic  10.9 us (2%)
    all_gather x1, waiting for transfers between devices, body(): portion = lax.all_gather(spectra_pair, 'feat', axis=2, tiled=True)  193 us
    all_gather x1, waiting for transfers between devices, body(): lax.all_gather(features, 'feat', axis=0, tiled=True)  113 us
    reduce_scatter x1, waiting for transfers between devices, body(): lax.psum_scatter(partial_gram, 'dp', scatter_dimension=0, tiled=True)  38.7 us
    psum x1, blocking collectives, body(): target_sum = lax.psum(target_part, 'dp')  29.1 us
    dot_general x1, matrix products, inverse_terms(): jnp.einsum('fc,rf->cr', sine, spectra_pair[1], preferred_element_type=jnp...  21.4 us
    dot_general x1, matrix products, inverse_terms(): jnp.einsum('fc,rf->cr', cosine, spectra_pair[0], preferred_element_type=j...  21.1 us
  transfers between devices with their start and end apart: 3, of which 3 were waited for; matrix products, arithmetic and copies ran while one was open for 0% of the time, Pallas kernels for 0%

commit v1 on v0

v1 whole, which is shorter than its diff:
```python
import functools, math
import jax, jax.numpy as jnp
from jax import lax
from jax.experimental import pallas as pl
from jax.experimental.pallas import tpu as pltpu
from jax.sharding import PartitionSpec as P

F32, BF, I32 = jnp.float32, jnp.bfloat16, jnp.int32
SK = 4096

def sin_poly(t):
    u = t * t
    p = jnp.float32(2.6019031e-06)
    p = p * u + jnp.float32(-1.9807414e-04)
    p = p * u + jnp.float32(8.3330255e-03)
    p = p * u + jnp.float32(-1.6666657e-01)
    return t + t * (u * p)

def sin_turn(n, period):
    quarter = period // 4
    m = ((n + quarter) & (period - 1)) - quarter
    m = jnp.where(m > quarter, period // 2 - m, m)
    return sin_poly(m.astype(F32) * jnp.float32(2.0 * math.pi / period))

def cos_turn(n, period):
    return sin_turn(n + period // 4, period)

def iota(shape, dim):
    return lax.broadcasted_iota(I32, shape, dim)

def setup(bid_ref, sign_ref, e_ref, step_ref, base_ref):
    for k in range(3):
        packed = bid_ref[k:k + 1, :] + SK * sign_ref[k:k + 1, :]
        eye = iota((256, 256), 0) == iota((256, 256), 1)
        column = jnp.sum(jnp.where(eye, packed.astype(F32), 0.0), axis=1, keepdims=True)
        column = jnp.broadcast_to(column, (256, 128)).astype(I32)
        b = column & (SK - 1)
        s = (2 * (column >> 12) - 1).astype(F32)
        step_ref[k, 0] = cos_turn(b, SK)
        step_ref[k, 1] = -sin_turn(b, SK)
        for half in range(2):
            f2 = iota((256, 128), 1) + 128 * half
            n = b * f2
            e_ref[k, 0, :, 128 * half:128 * half + 128] = s * cos_turn(n, 256)
            e_ref[k, 1, :, 128 * half:128 * half + 128] = -s * sin_turn(n, 256)
    n = iota((256, 256), 0) * iota((256, 256), 1)
    base_ref[0] = cos_turn(n, 256)
    base_ref[1] = sin_turn(n, 256)

def put_split(t_ref, col, value):
    hi = value.astype(BF)
    t_ref[0:256, col:col + value.shape[1]] = hi
    t_ref[256:512, col:col + value.shape[1]] = (value - hi.astype(F32)).astype(BF)

def table_first(e_ref, step_ref, t_ref):
    for k in range(3):
        sr, si = step_ref[k, 0], step_ref[k, 1]
        er, ei = e_ref[k, 0, :, 0:128], e_ref[k, 1, :, 0:128]
        s2r, s2i = sr * sr - si * si, 2.0 * sr * si
        s4r, s4i = s2r * s2r - s2i * s2i, 2.0 * s2r * s2i
        s8r, s8i = s4r * s4r - s4i * s4i, 2.0 * s4r * s4i
        nyq = e_ref[k, 0, :, 128:256]
        lane = iota((256, 128), 1)
        nyq0 = jnp.sum(jnp.where(lane == 0, nyq, 0.0), axis=1, keepdims=True)
        put_split(t_ref, 512 * k, er)
        put_split(t_ref, 512 * k + 128, er * s8r - ei * s8i)
        put_split(t_ref, 512 * k + 256, jnp.where(lane == 0, nyq0, ei))
        put_split(t_ref, 512 * k + 384, er * s8i + ei * s8r)

def table_next(e_ref, step_ref, t_ref):
    for k in range(3):
        sr, si = step_ref[k, 0], step_ref[k, 1]
        for half in range(2):
            cols = slice(128 * half, 128 * half + 128)
            er, ei = e_ref[k, 0, :, cols], e_ref[k, 1, :, cols]
            nr, ni = er * sr - ei * si, er * si + ei * sr
            e_ref[k, 0, :, cols] = nr
            e_ref[k, 1, :, cols] = ni
            put_split(t_ref, 512 * k + 128 * half, nr)
            put_split(t_ref, 512 * k + 256 + 128 * half, ni)

def inverse_first(base_ref, w_ref):
    c2 = iota((8, 256), 1)[0:1]
    r8, i8 = cos_turn(8 * c2, SK), sin_turn(8 * c2, SK)
    c, s = base_ref[0, 0:128], base_ref[1, 0:128]
    first = iota((128, 256), 0) == 0
    gain = jnp.where(first, 1.0 / 64, 2.0 / 64)
    alt = (1 - 2 * (iota((128, 256), 1) & 1)).astype(F32)
    zero = jnp.zeros((128, 256), BF)
    w_ref[0:128, 0:256] = (c * gain).astype(BF)
    w_ref[0:128, 256:512] = zero
    w_ref[128:256, 0:256] = zero
    w_ref[128:256, 256:512] = ((c * r8 - s * i8) * (2.0 / 64)).astype(BF)
    w_ref[256:384, 0:256] = jnp.where(first, alt * (1.0 / 64), s * (-2.0 / 64)).astype(BF)
    w_ref[256:384, 256:512] = zero
    w_ref[384:512, 0:256] = zero
    w_ref[384:512, 256:512] = ((s * r8 + c * i8) * (-2.0 / 64)).astype(BF)

def inverse_next(g, base_ref, w_ref):
    c2 = iota((8, 256), 1)
    r, i = cos_turn(g * c2, SK)[0:1] * (2.0 / 64), sin_turn(g * c2, SK)[0:1] * (2.0 / 64)
    c, s = base_ref[0], base_ref[1]
    wr, wi = c * r - s * i, s * r + c * i
    w_ref[0:256, 0:256] = wr.astype(BF)
    w_ref[256:512, 256:512] = wr.astype(BF)
    w_ref[0:256, 256:512] = wi.astype(BF)
    w_ref[256:512, 0:256] = (-wi).astype(BF)

def multiply(rows, first, spec_ref, cube_ref, p_ref):
    block = 16
    def step(i, carry):
        r = pl.ds(pl.multiple_of(i * block, block), block)
        cube = cube_ref[r, :]
        for half in range(2):
            def part(col):
                return spec_ref[r, col + 128 * half:col + 128 * half + 128]
            ar, ai, br, bi, cr, ci = [part(256 * q) for q in range(6)]
            ar, ai = ar * cube, ai * cube
            xr, xi = ar * br - ai * bi, ar * bi + ai * br
            yr, yi = xr * cr - xi * ci, xr * ci + xi * cr
            if first and half == 0:
                lane = iota((block, 128), 1) == 0
                yr = jnp.where(lane, ar * br * cr, yr)
                yi = jnp.where(lane, ai * bi * ci, yi)
            p_ref[r, 128 * half:128 * half + 128] = yr.astype(BF)
            p_ref[r, 256 + 128 * half:256 + 128 * half + 128] = yi.astype(BF)
        return carry
    lax.fori_loop(0, rows // block, step, 0, unroll=5 if (rows // block) % 5 == 0 else 4)

def combine(rows, y_ref, f_ref):
    block = 16
    h, C, S = (jnp.float32(v) for v in (math.sqrt(0.5), math.cos(math.pi / 8), math.sin(math.pi / 8)))
    def step(n, carry):
        r = pl.ds(pl.multiple_of(n * block, block), block)
        for half in range(2):
            lo = slice(128 * half, 128 * half + 128)
            hi = slice(256 + 128 * half, 256 + 128 * half + 128)
            out = [None] * 16
            re = lambda g: y_ref[g, r, lo]
            im = lambda g: y_ref[g, r, hi]
            y0, y8 = re(0), im(0)
            a, b = y0 + y8, y0 - y8
            r4, i4 = re(4), im(4)
            ee = [a + r4, b - i4, a - r4, b + i4]
            r2, i2, r6, i6 = re(2), im(2), re(6), im(6)
            d, e = h * (r2 - r6), h * (i2 + i6)
            eo = [r2 + r6, d - e, i6 - i2, -d - e]
            even = [ee[q] + eo[q] for q in range(4)] + [ee[q] - eo[q] for q in range(4)]
            r1, r7, i1, i7 = re(1), re(7), im(1), im(7)
            r3, r5, i3, i5 = re(3), re(5), im(3), im(5)
            p1, m1, q1, n1 = r1 + r7, r1 - r7, i1 - i7, i1 + i7
            p3, m3, q3, n3 = r3 + r5, r3 - r5, i3 - i5, i3 + i5
            dp, dq = h * (p1 - p3), h * (q1 + q3)
            u1, v1 = m1 * C + m3 * S, n1 * S + n3 * C
            u3, v3 = m1 * S - m3 * C, n1 * C - n3 * S
            odd = [p1 + p3, u1 - v1, dp - dq, u3 - v3, q3 - q1, -u3 - v3, -dp - dq, -u1 - v1]
            for q in range(8):
                f_ref[q, r, lo] = (even[q] + odd[q]).astype(BF)
                f_ref[q + 8, r, lo] = (even[q] - odd[q]).astype(BF)
        return carry
    lax.fori_loop(0, rows // block, step, 0)

def features(rows, x2_ref, cube_ref, e_ref, step_ref, base_ref, t_ref, w_ref, spec_ref, p_ref, y_ref, f_ref):
    def dots(g, first):
        spec_ref[...] = jnp.dot(x2_ref[...], t_ref[...], preferred_element_type=F32)
        multiply(rows, first, spec_ref, cube_ref, p_ref)
        y_ref[g] = jnp.dot(p_ref[...], w_ref[...], preferred_element_type=F32)
    table_first(e_ref, step_ref, t_ref)
    inverse_first(base_ref, w_ref)
    dots(0, True)
    def step(g, carry):
        table_next(e_ref, step_ref, t_ref)
        inverse_next(g, base_ref, w_ref)
        dots(g, False)
        return carry
    lax.fori_loop(1, 8, step, 0)
    combine(rows, y_ref, f_ref)


def sketch_kernel(rows, x_ref, target_ref, count_ref, bid_ref, sign_ref, g_ref, z_ref,
                  x2, cube, e_ref, step_ref, base_ref, t_ref, w_ref, spec, p_ref, y_ref, f_ref):
    live = count_ref[lax.axis_index("dp")]
    xf = jnp.where(iota((rows, 256), 0) < live, x_ref[...].astype(F32), 0.0)
    s = lax.rsqrt(jnp.mean(xf * xf, axis=1, keepdims=True) + 1e-6) * (1.0 / 16)
    cube[...] = jnp.broadcast_to(s * s * s, (rows, 128))
    x2[:, 0:256] = xf.astype(BF)
    x2[:, 256:512] = xf.astype(BF)
    setup(bid_ref, sign_ref, e_ref, step_ref, base_ref)
    features(rows, x2, cube, e_ref, step_ref, base_ref, t_ref, w_ref, spec, p_ref, y_ref, f_ref)
    own = f_ref[lax.axis_index("feat")]
    turned = own.astype(F32).T.astype(BF)
    target = jnp.broadcast_to(target_ref[...].astype(F32), (8, rows)).astype(BF)
    z_ref[...] = jnp.dot(target, own, preferred_element_type=F32)

    def step(i, carry):
        g_ref[i] = jnp.dot(turned, f_ref[i], preferred_element_type=F32).astype(BF)
        return carry

    lax.fori_loop(0, 16, step, 0)


def sketch_call(rows):
    vmem = pl.BlockSpec(memory_space=pltpu.VMEM)
    return pl.pallas_call(
        functools.partial(sketch_kernel, rows),
        out_shape=(jax.ShapeDtypeStruct((16, 256, 256), BF), jax.ShapeDtypeStruct((8, 256), F32)),
        in_specs=[vmem, vmem, pl.BlockSpec(memory_space=pltpu.SMEM), vmem, vmem],
        out_specs=[vmem, vmem],
        scratch_shapes=[
            pltpu.VMEM((rows, 512), BF),
            pltpu.VMEM((rows, 128), F32),
            pltpu.VMEM((3, 2, 256, 256), F32),
            pltpu.VMEM((3, 2, 256, 128), F32),
            pltpu.VMEM((2, 256, 256), F32),
            pltpu.VMEM((512, 1536), BF),
            pltpu.VMEM((512, 512), BF),
            pltpu.VMEM((rows, 1536), F32),
            pltpu.VMEM((rows, 512), BF),
            pltpu.VMEM((8, rows, 512), F32),
            pltpu.VMEM((16, rows, 256), BF),
        ],
        compiler_params=pltpu.CompilerParams(vmem_limit_bytes=58 << 20),
        name="sketch",
    )


MESH = pl.DeviceIdType.MESH
FLOWS = ((2, 1), (2, 0), (1, 1), (3, 1), (1, 0), (3, 0), (0, 1))


def scatter_kernel(g_ref, z_ref, gram_ref, zty_ref, sib, sibz, tx, rx, zall,
                   sib_send, sib_recv, send, recv, z_send, z_recv):
    d = lax.axis_index("dp")
    core, chip = d % 2, d // 2
    lane, ring = chip % 2, chip // 2
    sibling = 2 * chip + 1 - core

    def chip_at(flow):
        return 2 * ((ring + flow[0]) % 4) + (lane + flow[1]) % 2

    barrier = pltpu.get_barrier_semaphore()
    peers = [sibling] + [2 * chip_at(flow) + core for flow in FLOWS]
    for peer in peers:
        pl.semaphore_signal(barrier, inc=1, device_id={"dp": peer}, device_id_type=MESH)
    pl.semaphore_wait(barrier, len(peers))

    order = [chip_at(flow) for flow in FLOWS] + [chip]
    pair = []
    for i, q in enumerate(order):
        copy = pltpu.make_async_remote_copy(
            src_ref=g_ref.at[2 * q + 1 - core], dst_ref=sib.at[i], send_sem=sib_send.at[i],
            recv_sem=sib_recv.at[i], device_id={"dp": sibling}, device_id_type=MESH)
        copy.start()
        pair.append(copy)
    zcopy = pltpu.make_async_remote_copy(
        src_ref=z_ref, dst_ref=sibz, send_sem=sib_send.at[8], recv_sem=sib_recv.at[8],
        device_id={"dp": sibling}, device_id_type=MESH)
    zcopy.start()

    sends = []
    for i in range(7):
        pair[i].wait_recv()
        tx[i] = (g_ref[2 * order[i] + core].astype(F32) + sib[i].astype(F32)).astype(BF)
        copy = pltpu.make_async_remote_copy(
            src_ref=tx.at[i], dst_ref=rx.at[i], send_sem=send.at[i], recv_sem=recv.at[i],
            device_id={"dp": peers[1 + i]}, device_id_type=MESH)
        copy.start()
        sends.append(copy)
    zcopy.wait_recv()
    zall[chip] = z_ref[...] + sibz[...]
    for i in range(7):
        copy = pltpu.make_async_remote_copy(
            src_ref=zall.at[chip], dst_ref=zall.at[chip], send_sem=z_send.at[i], recv_sem=z_recv.at[i],
            device_id={"dp": peers[1 + i]}, device_id_type=MESH)
        copy.start()
        sends.append(copy)
    pair[7].wait_recv()
    total = g_ref[2 * chip + core].astype(F32) + sib[7].astype(F32)
    for i in (6, 5, 4, 3, 2, 1, 0):
        sends[i].wait_recv()
        total = total + rx[i].astype(F32)
    gram_ref[...] = total.T * jnp.float32(1.0 / 6144)
    for i in range(7):
        sends[7 + i].wait_recv()
    zty = zall[0]
    for i in range(1, 8):
        zty = zty + zall[i]
    zty_ref[...] = zty * jnp.float32(6144 ** -0.5)
    for copy in pair + [zcopy] + sends:
        copy.wait_send()


def scatter_call():
    vmem = pl.BlockSpec(memory_space=pltpu.VMEM)
    dma = pltpu.SemaphoreType.DMA
    return pl.pallas_call(
        scatter_kernel,
        out_shape=(jax.ShapeDtypeStruct((256, 256), F32), jax.ShapeDtypeStruct((8, 256), F32)),
        in_specs=[vmem, vmem],
        out_specs=[vmem, vmem],
        scratch_shapes=[
            pltpu.VMEM((8, 256, 256), BF),
            pltpu.VMEM((8, 256), F32),
            pltpu.VMEM((7, 256, 256), BF),
            pltpu.VMEM((7, 256, 256), BF),
            pltpu.VMEM((8, 8, 256), F32),
            dma((9,)), dma((9,)), dma((7,)), dma((7,)), dma((7,)), dma((7,)),
        ],
        compiler_params=pltpu.CompilerParams(
            collective_id=0, has_side_effects=True, vmem_limit_bytes=24 << 20),
        name="scatter",
    )


def body(samples, targets, counts, bucket_ids, sign_bits):
    rows = samples.shape[0]
    partial, zpart = sketch_call(rows)(
        samples, targets.reshape(1, rows), counts, bucket_ids, sign_bits)
    gram, zty = scatter_call()(partial, zpart)
    return gram, zty[0]


def solution(mesh):
    placed = (P("dp", None), P("dp"), P(), P(), P())
    return jax.shard_map(
        body, mesh=mesh, in_specs=placed, out_specs=(P("dp", "feat"), P("feat")), check_vma=False
    )
```

time: 457 us -> 61.2 us (0.13)
  waiting for transfers between devices: 345 us -> 0 us
  Pallas kernels: 0 us -> 55.5 us
  matrix products: 54.6 us -> 0 us
  blocking collectives: 29.1 us -> 0 us
  between operations: 13.8 us -> 0.64 us
  other arithmetic: 10.9 us -> 0 us
    all_gather x2 -> x0, waiting for transfers between devices: 306 us -> none  [the longest x1 193 us: body(): portion = lax.all_gather(spectra_pair, 'feat', axis=2, tiled=True)]
    pallas_call x0 -> x2, Pallas kernels: none -> 55.5 us  [the longest x1 34.3 us: body(): sketch_call(rows)]
    dot_general x5 -> x0, matrix products: 54.6 us -> none  [the longest x1 21.4 us: inverse_terms(): jnp.einsum('fc,rf->cr', sine, spectra_pair[1], preferred_element_type=jnp...]
    reduce_scatter x1 -> x0, waiting for transfers between devices: 38.7 us -> none  [body(): lax.psum_scatter(partial_gram, 'dp', scatter_dimension=0, tiled=True)]
    psum x1 -> x0, blocking collectives: 29.1 us -> none  [body(): target_sum = lax.psum(target_part, 'dp')]
  transfers between devices with their start and end apart: 3 -> 0, of which waited for: 3 -> 0; matrix products, arithmetic and copies ran while one was open for 0% -> 0% of each run, Pallas kernels for 0% -> 0%
where the time goes in v1:
time: 61.2 us; the launch traced here: 61 us
  Pallas kernels  55.5 us (91%)
  local copies, waits for them, and re-layouts  4.83 us (8%)
  between operations  0.64 us (1%)
    pallas_call x1, Pallas kernels, body(): sketch_call(rows)  34.3 us
    pallas_call x1, Pallas kernels, body(): gram, zty = scatter_call()(partial, zpart)  21.2 us
    unnamed x5, local copies, waits for them, and re-layouts  2.99 us
    reshape x1, local copies, waits for them, and re-layouts, body(): targets.reshape(1, rows)  1.28 us

profile of v1, /device:TPU:1, one launch (start us, length us, event | category | flops | bytes accessed | tf_op | source)
XLA Modules:
  0.0 61.0 jit_solution(12612371178290368918)
XLA Ops:
  0.6 1.3 %reshape.7.target_ref = bf16[1,768]{1,0:T(2,128)(2,1)} reshape(bf16[768]{0:T(1024)(128)(2,1)} %param.6) | data formatting | bytes 3072 | tf_op jit(solution)/shard_map/reshape | solution.py:318
  1.9 34.3 %sketch.1 = (bf16[16,256,256]{2,1,0:T(8,128)(2,1)}, f32[8,256]{1,0:T(8,128)}) custom-call(bf16[768,256]{1,0:T(8,128)(2,1)} %x_ref.1, bf16[1,768]{1,0:T(2,128)(2,1)} %reshape.7.target_ref, s32[16]{0:T(128)} %count_ref.1, s32[3,256]{1,0:T(4,128)} %bid_ref.1, s32[3,256]{1,0:T(4,128)} %sign_ref.1), custom_call_target="tpu_custom_call" | custom-call | tf_op jit(solution)/shard_map/sketch/pallas_call | solution.py:317
  36.2 0.0 copy-start
  36.2 1.6 %copy-done = bf16[16,256,256]{2,1,0:T(8,128)(2,1)S(1)} copy-done((bf16[16,256,256]{2,1,0:T(8,128)(2,1)S(1)}, bf16[16,256,256]{2,1,0:T(8,128)(2,1)}, u32[]{:S(2)}) %copy-start) | copy-done | bytes 2097176
  37.8 0.0 copy-start.1
  37.8 0.7 %copy-done.1 = f32[8,256]{1,0:T(8,128)S(1)} copy-done((f32[8,256]{1,0:T(8,128)S(1)}, f32[8,256]{1,0:T(8,128)}, u32[]{:S(2)}) %copy-start.1) | copy-done | bytes 8216
  38.5 21.2 %scatter.1 = (f32[256,256]{1,0:T(8,128)S(1)}, f32[8,256]{1,0:T(8,128)S(1)}) custom-call(bf16[16,256,256]{2,1,0:T(8,128)(2,1)S(1)} %copy-done, f32[8,256]{1,0:T(8,128)S(1)} %copy-done.1), custom_call_target="tpu_custom_call" | custom-call | tf_op jit(solution)/shard_map/scatter/pallas_call | solution.py:319
  59.7 0.6 slice.3
  60.3 0.7 %copy.8 = f32[256,256]{1,0:T(8,128)} copy(f32[256,256]{1,0:T(8,128)S(1)} %get-tuple-element.12) | data formatting | bytes 524288
Async XLA Ops:
  36.2 1.6 %copy-start = (bf16[16,256,256]{2,1,0:T(8,128)(2,1)S(1)}, bf16[16,256,256]{2,1,0:T(8,128)(2,1)}, u32[]{:S(2)}) copy-start(bf16[16,256,256]{2,1,0:T(8,128)(2,1)} %get-tuple-element.6.g_ref) | copy-start | bytes 6291460
  37.8 0.7 %copy-start.1 = (f32[8,256]{1,0:T(8,128)S(1)}, f32[8,256]{1,0:T(8,128)}, u32[]{:S(2)}) copy-start(f32[8,256]{1,0:T(8,128)} %get-tuple-element.7.z_ref) | copy-start | bytes 24580

commit v2 on v1

v2 whole, which is shorter than its diff:
```python
import functools, math
import jax, jax.numpy as jnp
from jax import lax
from jax.experimental import pallas as pl
from jax.experimental.pallas import tpu as pltpu
from jax.sharding import PartitionSpec as P

F32, BF, I32 = jnp.float32, jnp.bfloat16, jnp.int32
SK = 4096


def sin_poly(t):
    u = t * t
    p = jnp.float32(2.6019031e-06)
    p = p * u + jnp.float32(-1.9807414e-04)
    p = p * u + jnp.float32(8.3330255e-03)
    p = p * u + jnp.float32(-1.6666657e-01)
    return t + t * (u * p)


def sin_turn(n, period):
    quarter = period // 4
    m = ((n + quarter) & (period - 1)) - quarter
    m = jnp.where(m > quarter, period // 2 - m, m)
    return sin_poly(m.astype(F32) * jnp.float32(2.0 * math.pi / period))


def cos_turn(n, period):
    return sin_turn(n + period // 4, period)


def iota(shape, dim):
    return lax.broadcasted_iota(I32, shape, dim)


def setup(bid_ref, sign_ref, e_ref, step_ref, base_ref):
    for k in range(3):
        packed = bid_ref[k:k + 1, :] + SK * sign_ref[k:k + 1, :]
        eye = iota((256, 256), 0) == iota((256, 256), 1)
        column = jnp.sum(jnp.where(eye, packed.astype(F32), 0.0), axis=1, keepdims=True)
        column = jnp.broadcast_to(column, (256, 128)).astype(I32)
        b = column & (SK - 1)
        s = (2 * (column >> 12) - 1).astype(F32)
        step_ref[k, 0] = cos_turn(b, SK)
        step_ref[k, 1] = -sin_turn(b, SK)
        for half in range(2):
            n = b * (iota((256, 128), 1) + 128 * half)
            e_ref[k, half, 0] = s * cos_turn(n, 256)
            e_ref[k, half, 1] = -s * sin_turn(n, 256)
    n = iota((256, 256), 0) * iota((256, 256), 1)
    base_ref[0] = cos_turn(n, 256)
    base_ref[1] = sin_turn(n, 256)


def put_split(t_ref, col, value):
    hi = value.astype(BF)
    t_ref[0:256, col:col + 128] = hi
    t_ref[256:512, col:col + 128] = (value - hi.astype(F32)).astype(BF)


def table_first(e_ref, step_ref, ta, tb):
    for k in range(3):
        sr, si = step_ref[k, 0], step_ref[k, 1]
        er, ei = e_ref[k, 0, 0], e_ref[k, 0, 1]
        s2r, s2i = sr * sr - si * si, 2.0 * sr * si
        s4r, s4i = s2r * s2r - s2i * s2i, 2.0 * s2r * s2i
        s8r, s8i = s4r * s4r - s4i * s4i, 2.0 * s4r * s4i
        lane = iota((256, 128), 1)
        nyq = jnp.sum(jnp.where(lane == 0, e_ref[k, 1, 0], 0.0), axis=1, keepdims=True)
        put_split(ta, 256 * k, er)
        put_split(ta, 256 * k + 128, jnp.where(lane == 0, nyq, ei))
        put_split(tb, 256 * k, er * s8r - ei * s8i)
        put_split(tb, 256 * k + 128, er * s8i + ei * s8r)


def table_next(half, e_ref, step_ref, t_ref):
    for k in range(3):
        sr, si = step_ref[k, 0], step_ref[k, 1]
        er, ei = e_ref[k, half, 0], e_ref[k, half, 1]
        nr, ni = er * sr - ei * si, er * si + ei * sr
        e_ref[k, half, 0] = nr
        e_ref[k, half, 1] = ni
        put_split(t_ref, 256 * k, nr)
        put_split(t_ref, 256 * k + 128, ni)


def inverse_first(base_ref, w_ref):
    c2 = iota((8, 256), 1)
    r8, i8 = cos_turn(8 * c2, SK)[0:1], sin_turn(8 * c2, SK)[0:1]
    c, s = base_ref[0, 0:128], base_ref[1, 0:128]
    first = iota((128, 256), 0) == 0
    gain = jnp.where(first, 1.0 / 64, 2.0 / 64)
    alt = (1 - 2 * (iota((128, 256), 1) & 1)).astype(F32)
    zero = jnp.zeros((128, 256), BF)
    w_ref[0:128, 0:256] = (c * gain).astype(BF)
    w_ref[0:128, 256:512] = zero
    w_ref[128:256, 0:256] = jnp.where(first, alt * (1.0 / 64), s * (-2.0 / 64)).astype(BF)
    w_ref[128:256, 256:512] = zero
    w_ref[256:384, 0:256] = zero
    w_ref[256:384, 256:512] = ((c * r8 - s * i8) * (2.0 / 64)).astype(BF)
    w_ref[384:512, 0:256] = zero
    w_ref[384:512, 256:512] = ((s * r8 + c * i8) * (-2.0 / 64)).astype(BF)


def inverse_next(g, base_ref, w_ref):
    c2 = iota((8, 256), 1)
    r, i = cos_turn(g * c2, SK)[0:1] * (2.0 / 64), sin_turn(g * c2, SK)[0:1] * (2.0 / 64)
    for half in range(2):
        c, s = base_ref[0, 128 * half:128 * half + 128], base_ref[1, 128 * half:128 * half + 128]
        wr, wi = c * r - s * i, s * r + c * i
        w_ref[256 * half:256 * half + 128, 0:256] = wr.astype(BF)
        w_ref[256 * half:256 * half + 128, 256:512] = wi.astype(BF)
        w_ref[256 * half + 128:256 * half + 256, 0:256] = (-wi).astype(BF)
        w_ref[256 * half + 128:256 * half + 256, 256:512] = wr.astype(BF)


def multiply(rows, first, spec_ref, cube_ref, p_ref, half):
    block = 16
    for n in range(rows // block):
        r = slice(block * n, block * n + block)
        cube = cube_ref[r, :]
        ar, ai, br, bi, cr, ci = [spec_ref[r, 128 * q:128 * q + 128] for q in range(6)]
        ar, ai = ar * cube, ai * cube
        xr, xi = ar * br - ai * bi, ar * bi + ai * br
        yr, yi = xr * cr - xi * ci, xr * ci + xi * cr
        if first:
            lane = iota((block, 128), 1) == 0
            yr = jnp.where(lane, ar * br * cr, yr)
            yi = jnp.where(lane, ai * bi * ci, yi)
        p_ref[r, 256 * half:256 * half + 128] = yr.astype(BF)
        p_ref[r, 256 * half + 128:256 * half + 256] = yi.astype(BF)


def combine(rows, y_ref, f_ref):
    block = 16
    h, C, S = (jnp.float32(v) for v in (math.sqrt(0.5), math.cos(math.pi / 8), math.sin(math.pi / 8)))

    def step(n, carry):
        r = pl.ds(pl.multiple_of(n * block, block), block)
        for half in range(2):
            lo = slice(128 * half, 128 * half + 128)
            hi = slice(256 + 128 * half, 256 + 128 * half + 128)
            re = lambda g: y_ref[g, r, lo]
            im = lambda g: y_ref[g, r, hi]
            y0, y8 = re(0), im(0)
            a, b = y0 + y8, y0 - y8
            r4, i4 = re(4), im(4)
            ee = [a + r4, b - i4, a - r4, b + i4]
            r2, i2, r6, i6 = re(2), im(2), re(6), im(6)
            d, e = h * (r2 - r6), h * (i2 + i6)
            eo = [r2 + r6, d - e, i6 - i2, -d - e]
            even = [ee[q] + eo[q] for q in range(4)] + [ee[q] - eo[q] for q in range(4)]
            r1, r7, i1, i7 = re(1), re(7), im(1), im(7)
            r3, r5, i3, i5 = re(3), re(5), im(3), im(5)
            p1, m1, q1, n1 = r1 + r7, r1 - r7, i1 - i7, i1 + i7
            p3, m3, q3, n3 = r3 + r5, r3 - r5, i3 - i5, i3 + i5
            dp, dq = h * (p1 - p3), h * (q1 + q3)
            u1, v1 = m1 * C + m3 * S, n1 * S + n3 * C
            u3, v3 = m1 * S - m3 * C, n1 * C - n3 * S
            odd = [p1 + p3, u1 - v1, dp - dq, u3 - v3, q3 - q1, -u3 - v3, -dp - dq, -u1 - v1]
            for q in range(8):
                f_ref[q, r, lo] = (even[q] + odd[q]).astype(BF)
                f_ref[q + 8, r, lo] = (even[q] - odd[q]).astype(BF)
        return carry

    lax.fori_loop(0, rows // block, step, 0)


def dot(a, b):
    return jnp.dot(a, b, preferred_element_type=F32)


def features(rows, x2, cube, e_ref, step_ref, base_ref, ta, tb, w_ref, sa, sb, p_ref, y_ref, f_ref):
    table_first(e_ref, step_ref, ta, tb)
    sa[...] = dot(x2[...], ta[...])
    inverse_first(base_ref, w_ref)
    sb[...] = dot(x2[...], tb[...])
    multiply(rows, True, sa, cube, p_ref, 0)
    table_next(0, e_ref, step_ref, ta)

    def step(g, carry):
        sa[...] = dot(x2[...], ta[...])
        multiply(rows, False, sb, cube, p_ref, 1)
        table_next(1, e_ref, step_ref, tb)
        y_ref[g - 1] = dot(p_ref[...], w_ref[...])
        sb[...] = dot(x2[...], tb[...])
        multiply(rows, False, sa, cube, p_ref, 0)
        table_next(0, e_ref, step_ref, ta)
        inverse_next(g, base_ref, w_ref)
        return carry

    lax.fori_loop(1, 8, step, 0)
    multiply(rows, False, sb, cube, p_ref, 1)
    y_ref[7] = dot(p_ref[...], w_ref[...])
    combine(rows, y_ref, f_ref)


def scratch(rows):
    return [
        pltpu.VMEM((rows, 512), BF),
        pltpu.VMEM((rows, 128), F32),
        pltpu.VMEM((3, 2, 2, 256, 128), F32),
        pltpu.VMEM((3, 2, 256, 128), F32),
        pltpu.VMEM((2, 256, 256), F32),
        pltpu.VMEM((512, 768), BF),
        pltpu.VMEM((512, 768), BF),
        pltpu.VMEM((512, 512), BF),
        pltpu.VMEM((rows, 768), F32),
        pltpu.VMEM((rows, 768), F32),
        pltpu.VMEM((rows, 512), BF),
        pltpu.VMEM((8, rows, 512), F32),
        pltpu.VMEM((16, rows, 256), BF),
    ]


MESH = pl.DeviceIdType.MESH
FLOWS = ((2, 1), (2, 0), (1, 1), (3, 1), (1, 0), (3, 0), (0, 1))


def fused_kernel(rows, x_ref, target_ref, count_ref, bid_ref, sign_ref, gram_ref, zty_ref,
                 x2, cube, e_ref, step_ref, base_ref, ta, tb, w_ref, sa, sb, p_ref, y_ref, f_ref,
                 half, mine, sib, tx, rx, zown, sibz, zall,
                 sib_send, sib_recv, send, recv, z_send, z_recv):
    d = lax.axis_index("dp")
    core, chip = d % 2, d // 2
    lane, ring = chip % 2, chip // 2
    sibling = 2 * chip + 1 - core

    def chip_at(flow):
        return 2 * ((ring + flow[0]) % 4) + (lane + flow[1]) % 2

    order = [chip_at(flow) for flow in FLOWS] + [chip]
    peers = [2 * q + core for q in order[:7]]
    barrier = pltpu.get_barrier_semaphore()
    for peer in [sibling] + peers:
        pl.semaphore_signal(barrier, inc=1, device_id={"dp": peer}, device_id_type=MESH)

    def remote(src, dst, send_sem, recv_sem, peer):
        return pltpu.make_async_remote_copy(
            src_ref=src, dst_ref=dst, send_sem=send_sem, recv_sem=recv_sem,
            device_id={"dp": peer}, device_id_type=MESH)

    live = count_ref[d]
    xf = jnp.where(iota((rows, 256), 0) < live, x_ref[...].astype(F32), 0.0)
    s = lax.rsqrt(jnp.mean(xf * xf, axis=1, keepdims=True) + 1e-6) * (1.0 / 16)
    cube[...] = jnp.broadcast_to(s * s * s, (rows, 128))
    x2[:, 0:256] = xf.astype(BF)
    x2[:, 256:512] = xf.astype(BF)
    setup(bid_ref, sign_ref, e_ref, step_ref, base_ref)
    features(rows, x2, cube, e_ref, step_ref, base_ref, ta, tb, w_ref, sa, sb, p_ref, y_ref, f_ref)

    own = f_ref[lax.axis_index("feat")]
    target = jnp.concatenate(
        [jnp.broadcast_to(target_ref[n:n + 1, :].astype(F32), (8, 128)) for n in range(rows // 128)],
        axis=1).astype(BF)
    zown[...] = dot(target, own)
    turned = own.astype(F32).T.astype(BF)
    pl.semaphore_wait(barrier, 8)
    zcopy = remote(zown, sibz, sib_send.at[8], sib_recv.at[8], sibling)
    pair = [remote(half.at[i], sib.at[i], sib_send.at[i], sib_recv.at[i], sibling) for i in range(8)]
    sends = [remote(tx.at[i], rx.at[i], send.at[i], recv.at[i], peers[i]) for i in range(7)]
    zsends = [remote(zall.at[chip], zall.at[chip], z_send.at[i], z_recv.at[i], peers[i]) for i in range(7)]

    for i, q in enumerate(order):
        half[i] = dot(turned, f_ref[2 * q + 1 - core]).astype(BF)
        if i == 0:
            zcopy.start()
        if i >= 2:
            sends[i - 2].start()
        mine[i] = dot(turned, f_ref[2 * q + core])
        pair[i].start()
        if i >= 1:
            pair[i - 1].wait_recv()
            tx[i - 1] = (mine[i - 1] + sib[i - 1].astype(F32)).astype(BF)
        if i == 2:
            zcopy.wait_recv()
            zall[chip] = zown[...] + sibz[...]
    sends[6].start()
    for copy in zsends:
        copy.start()
    pair[7].wait_recv()
    total = mine[7] + sib[7].astype(F32)
    for i in (6, 5, 4, 3, 2, 1, 0):
        sends[i].wait_recv()
        total = total + rx[i].astype(F32)
    gram_ref[...] = total.T * jnp.float32(1.0 / 6144)
    for copy in zsends:
        copy.wait_recv()
    zty = zall[0]
    for i in range(1, 8):
        zty = zty + zall[i]
    zty_ref[...] = zty[0:1] * jnp.float32(6144 ** -0.5)
    for copy in pair + [zcopy] + sends + zsends:
        copy.wait_send()


def fused_call(rows):
    vmem = pl.BlockSpec(memory_space=pltpu.VMEM)
    dma = pltpu.SemaphoreType.DMA
    return pl.pallas_call(
        functools.partial(fused_kernel, rows),
        out_shape=(jax.ShapeDtypeStruct((256, 256), F32), jax.ShapeDtypeStruct((1, 256), F32)),
        in_specs=[vmem, vmem, pl.BlockSpec(memory_space=pltpu.SMEM), vmem, vmem],
        out_specs=[vmem, vmem],
        scratch_shapes=scratch(rows) + [
            pltpu.VMEM((8, 256, 256), BF),
            pltpu.VMEM((8, 256, 256), F32),
            pltpu.VMEM((8, 256, 256), BF),
            pltpu.VMEM((7, 256, 256), BF),
            pltpu.VMEM((7, 256, 256), BF),
            pltpu.VMEM((8, 256), F32),
            pltpu.VMEM((8, 256), F32),
            pltpu.VMEM((8, 8, 256), F32),
            dma((9,)), dma((9,)), dma((7,)), dma((7,)), dma((7,)), dma((7,)),
        ],
        compiler_params=pltpu.CompilerParams(
            collective_id=0, has_side_effects=True, vmem_limit_bytes=58 << 20),
        name="fused",
    )


def body(samples, targets, counts, bucket_ids, sign_bits):
    rows = samples.shape[0]
    gram, zty = fused_call(rows)(
        samples, targets.reshape(rows // 128, 128), counts, bucket_ids, sign_bits)
    return gram, zty.reshape(256)


def solution(mesh):
    placed = (P("dp", None), P("dp"), P(), P(), P())
    return jax.shard_map(
        body, mesh=mesh, in_specs=placed, out_specs=(P("dp", "feat"), P("feat")), check_vma=False
    )
```

time: 61.2 us -> 47.5 us (0.78)
  Pallas kernels: 55.5 us -> 44.5 us
  local copies, waits for them, and re-layouts: 4.83 us -> 2.24 us
    pallas_call x2 -> x1, Pallas kernels: 55.5 us -> 44.5 us  [body(): fused_call(rows)]
    reshape x1 -> x0, local copies, waits for them, and re-layouts: 1.28 us -> none  [body(): targets.reshape(1, rows)]
    unnamed x5 -> x4, local copies, waits for them, and re-layouts: 2.99 us -> 2.24 us
where the time goes in v2:
time: 47.5 us; the launch traced here: 47.3 us
  Pallas kernels  44.5 us (94%)
  local copies, waits for them, and re-layouts  2.24 us (5%)
  between operations  0.65 us (1%)
    pallas_call x1, Pallas kernels, body(): fused_call(rows)  44.5 us
    unnamed x4, local copies, waits for them, and re-layouts  2.24 us

profile of v2, /device:TPU:1, one launch (start us, length us, event | category | flops | bytes accessed | tf_op | source)
XLA Modules:
  0.0 47.3 jit_solution(13253681599196297745)
XLA Ops:
  0.6 44.5 %fused.1 = (f32[256,256]{1,0:T(8,128)}, f32[1,256]{1,0:T(1,128)}) custom-call(bf16[768,256]{1,0:T(8,128)(2,1)} %x_ref.1, bf16[6,128]{1,0:T(8,128)(2,1)} %bitcast.2, s32[16]{0:T(128)} %count_ref.1, s32[3,256]{1,0:T(4,128)} %bid_ref.1, s32[3,256]{1,0:T(4,128)} %sign_ref.1), custom_call_target="tpu_custom_call" | custom-call | tf_op jit(solution)/shard_map/fused/pallas_call | solution.py:324
  45.1 0.0 copy-start
  45.1 1.7 %copy.9 = f32[256,256]{1,0:T(8,128)} copy(f32[256,256]{1,0:T(8,128)} %get-tuple-element.8) | data formatting | bytes 524288
  46.8 0.0 copy-done
  46.8 0.6 %copy.10 = f32[256]{0:T(256)} copy(f32[256]{0:T(256)S(1)} %bitcast.3) | data formatting | bytes 2048
Async XLA Ops:
  45.1 1.7 %copy-start = (f32[1,256]{1,0:T(1,128)S(1)}, f32[1,256]{1,0:T(1,128)}, u32[]{:S(2)}) copy-start(f32[1,256]{1,0:T(1,128)} %get-tuple-element.5) | copy-start | bytes 3076

commit v3 on v2

--- a/solution.py
+++ b/solution.py
@@ -213,26 +213,37 @@
     ]
 
 
+def sketch(rows, bid_ref, sign_ref, x2, cube, e_ref, step_ref, base_ref, ta, tb, w_ref, sa, sb, p_ref, y_ref, f_ref):
+    setup(bid_ref, sign_ref, e_ref, step_ref, base_ref)
+    features(rows, x2, cube, e_ref, step_ref, base_ref, ta, tb, w_ref, sa, sb, p_ref, y_ref, f_ref)
+
+
 MESH = pl.DeviceIdType.MESH
-FLOWS = ((2, 1), (2, 0), (1, 1), (3, 1), (1, 0), (3, 0), (0, 1))
-
-
-def fused_kernel(rows, x_ref, target_ref, count_ref, bid_ref, sign_ref, gram_ref, zty_ref,
-                 x2, cube, e_ref, step_ref, base_ref, ta, tb, w_ref, sa, sb, p_ref, y_ref, f_ref,
-                 half, mine, sib, tx, rx, zown, sibz, zall,
-                 sib_send, sib_recv, send, recv, z_send, z_recv):
+
+
+def fused_kernel(rows, x_hbm, target_hbm, count_hbm, bid_hbm, sign_hbm, gram_ref, zty_ref,
+                 x_ref, target_ref, count_ref, bid_ref, sign_ref, in_sem, *refs):
+    inputs = [pltpu.make_async_copy(src, dst, in_sem.at[i]) for i, (src, dst) in enumerate((
+        (bid_hbm, bid_ref), (sign_hbm, sign_ref), (count_hbm, count_ref), (x_hbm, x_ref), (target_hbm, target_ref)))]
+    for copy in inputs:
+        copy.start()
+    (half, mine, sib, tx, rx, zown, sibz, zpair, zx, zall,
+     sib_send, sib_recv, send, recv, z_send, z_recv) = refs[-16:]
+    x2, cube, f_ref = refs[0], refs[1], refs[-17]
     d = lax.axis_index("dp")
-    core, chip = d % 2, d // 2
-    lane, ring = chip % 2, chip // 2
-    sibling = 2 * chip + 1 - core
-
-    def chip_at(flow):
-        return 2 * ((ring + flow[0]) % 4) + (lane + flow[1]) % 2
-
-    order = [chip_at(flow) for flow in FLOWS] + [chip]
-    peers = [2 * q + core for q in order[:7]]
+    core, lane, ring = d % 2, (d // 2) % 2, d // 4
+
+    def device(turn, other):
+        return 4 * ((ring + turn) % 4) + 2 * ((lane + other) % 2) + core
+
+    def choose(first, second):
+        return first * (1 - core) + second * core
+
+    sibling = d + 1 - 2 * core
+    across, one, two, three = device(0, 1), device(1, 0), device(2, 0), device(3, 0)
+    neighbours = (sibling, across, one, two, three)
     barrier = pltpu.get_barrier_semaphore()
-    for peer in [sibling] + peers:
+    for peer in neighbours:
         pl.semaphore_signal(barrier, inc=1, device_id={"dp": peer}, device_id_type=MESH)
 
     def remote(src, dst, send_sem, recv_sem, peer):
@@ -240,14 +251,15 @@
             src_ref=src, dst_ref=dst, send_sem=send_sem, recv_sem=recv_sem,
             device_id={"dp": peer}, device_id_type=MESH)
 
+    for copy in inputs:
+        copy.wait()
     live = count_ref[d]
     xf = jnp.where(iota((rows, 256), 0) < live, x_ref[...].astype(F32), 0.0)
     s = lax.rsqrt(jnp.mean(xf * xf, axis=1, keepdims=True) + 1e-6) * (1.0 / 16)
     cube[...] = jnp.broadcast_to(s * s * s, (rows, 128))
     x2[:, 0:256] = xf.astype(BF)
     x2[:, 256:512] = xf.astype(BF)
-    setup(bid_ref, sign_ref, e_ref, step_ref, base_ref)
-    features(rows, x2, cube, e_ref, step_ref, base_ref, ta, tb, w_ref, sa, sb, p_ref, y_ref, f_ref)
+    sketch(rows, bid_ref, sign_ref, *refs[:-16])
 
     own = f_ref[lax.axis_index("feat")]
     target = jnp.concatenate(
@@ -255,42 +267,99 @@
         axis=1).astype(BF)
     zown[...] = dot(target, own)
     turned = own.astype(F32).T.astype(BF)
-    pl.semaphore_wait(barrier, 8)
-    zcopy = remote(zown, sibz, sib_send.at[8], sib_recv.at[8], sibling)
+    pl.semaphore_wait(barrier, len(neighbours))
+
+    lanes_first = ((2, 1), (1, 1), (3, 1), (0, 1), (2, 0), (1, 0), (3, 0), (0, 0))
+    rings_first = ((2, 1), (2, 0), (1, 1), (1, 0), (3, 1), (3, 0), (0, 1), (0, 0))
+    zero_chip = [(device(*at) - core) for at in lanes_first]
+    one_chip = [(device(*at) - core) for at in rings_first]
+    peers = [choose(a, b) for a, b in zip(
+        (across, across, across, across, two, one, three), (two, two, one, one, three, three, across))]
     pair = [remote(half.at[i], sib.at[i], sib_send.at[i], sib_recv.at[i], sibling) for i in range(8)]
-    sends = [remote(tx.at[i], rx.at[i], send.at[i], recv.at[i], peers[i]) for i in range(7)]
-    zsends = [remote(zall.at[chip], zall.at[chip], z_send.at[i], z_recv.at[i], peers[i]) for i in range(7)]
-
-    for i, q in enumerate(order):
-        half[i] = dot(turned, f_ref[2 * q + 1 - core]).astype(BF)
+    message = [remote(tx.at[i], rx.at[i], send.at[i], recv.at[i], peers[i]) for i in range(7)]
+    z_pair = remote(zown, sibz, z_send.at[0], z_recv.at[0], sibling)
+    z_lane = remote(zpair, zx, z_send.at[1], z_recv.at[1], across)
+    z_ring = [remote(zall.at[ring], zall.at[ring], z_send.at[2 + i], z_recv.at[2 + i], peer)
+              for i, peer in enumerate((one, two, three))]
+
+    def finish(k):
+        pair[k].wait_recv()
+        total = mine[k] + sib[k].astype(F32)
+        if k < 6:
+            tx[k] = total.astype(BF)
+        if k > 3:
+            mine[k] = total
+
+    def begin(k):
+        if k < 4:
+            message[k].start()
+        elif k < 6:
+            @pl.when(core == 1)
+            def _():
+                message[k].start()
+
+    for i in range(8):
+        half[i] = dot(turned, f_ref[choose(one_chip[i] + 1, zero_chip[i])]).astype(BF)
         if i == 0:
-            zcopy.start()
+            z_pair.start()
         if i >= 2:
-            sends[i - 2].start()
-        mine[i] = dot(turned, f_ref[2 * q + core])
+            begin(i - 2)
+        mine[i] = dot(turned, f_ref[choose(zero_chip[i], one_chip[i] + 1)])
         pair[i].start()
         if i >= 1:
-            pair[i - 1].wait_recv()
-            tx[i - 1] = (mine[i - 1] + sib[i - 1].astype(F32)).astype(BF)
-        if i == 2:
-            zcopy.wait_recv()
-            zall[chip] = zown[...] + sibz[...]
-    sends[6].start()
-    for copy in zsends:
-        copy.start()
-    pair[7].wait_recv()
-    total = mine[7] + sib[7].astype(F32)
-    for i in (6, 5, 4, 3, 2, 1, 0):
-        sends[i].wait_recv()
-        total = total + rx[i].astype(F32)
-    gram_ref[...] = total.T * jnp.float32(1.0 / 6144)
-    for copy in zsends:
+            finish(i - 1)
+        if i == 3:
+            z_pair.wait_recv()
+            zpair[...] = zown[...] + sibz[...]
+        if i == 4:
+            z_lane.start()
+    finish(7)
+
+    @pl.when(core == 0)
+    def _():
+        for k in range(3):
+            message[k].wait_recv()
+            tx[4 + k] = (mine[4 + k] + rx[k].astype(F32)).astype(BF)
+            if k > 0:
+                message[3 + k].start()
+        message[3].wait_recv()
+        mine[0] = mine[7] + rx[3].astype(F32)
+        message[6].start()
+
+    @pl.when(core == 1)
+    def _():
+        for k in (0, 2, 4):
+            message[k].wait_recv()
+        tx[6] = (mine[6] + rx[0].astype(F32) + rx[2].astype(F32) + rx[4].astype(F32)).astype(BF)
+        for k in (1, 3):
+            message[k].wait_recv()
+        mine[0] = mine[7] + rx[1].astype(F32) + rx[3].astype(F32)
+        message[6].start()
+
+    z_lane.wait_recv()
+    zall[ring] = zpair[...] + zx[...]
+
+    @pl.when(core == 0)
+    def _():
+        for copy in z_ring:
+            copy.start()
+        message[4].wait_recv()
+        message[5].wait_recv()
+        mine[0] = mine[0] + rx[4].astype(F32) + rx[5].astype(F32)
+
+    @pl.when(core == 1)
+    def _():
+        for copy in z_ring:
+            copy.start()
+        message[5].wait_recv()
+        mine[0] = mine[0] + rx[5].astype(F32)
+
+    for copy in z_ring:
         copy.wait_recv()
-    zty = zall[0]
-    for i in range(1, 8):
-        zty = zty + zall[i]
-    zty_ref[...] = zty[0:1] * jnp.float32(6144 ** -0.5)
-    for copy in pair + [zcopy] + sends + zsends:
+    zty_ref[...] = ((zall[0] + zall[1]) + (zall[2] + zall[3]))[0:1] * jnp.float32(6144 ** -0.5)
+    message[6].wait_recv()
+    gram_ref[...] = (mine[0] + rx[6].astype(F32)).T * jnp.float32(1.0 / 6144)
+    for copy in pair + message + [z_pair, z_lane] + z_ring:
         copy.wait_send()
 
 
@@ -300,9 +369,16 @@
     return pl.pallas_call(
         functools.partial(fused_kernel, rows),
         out_shape=(jax.ShapeDtypeStruct((256, 256), F32), jax.ShapeDtypeStruct((1, 256), F32)),
-        in_specs=[vmem, vmem, pl.BlockSpec(memory_space=pltpu.SMEM), vmem, vmem],
+        in_specs=[pl.BlockSpec(memory_space=pltpu.HBM)] * 5,
         out_specs=[vmem, vmem],
-        scratch_shapes=scratch(rows) + [
+        scratch_shapes=[
+            pltpu.VMEM((rows, 256), BF),
+            pltpu.VMEM((rows // 128, 128), BF),
+            pltpu.SMEM((16,), I32),
+            pltpu.VMEM((3, 256), I32),
+            pltpu.VMEM((3, 256), I32),
+            dma((5,)),
+        ] + scratch(rows) + [
             pltpu.VMEM((8, 256, 256), BF),
             pltpu.VMEM((8, 256, 256), F32),
             pltpu.VMEM((8, 256, 256), BF),
@@ -310,19 +386,22 @@
             pltpu.VMEM((7, 256, 256), BF),
             pltpu.VMEM((8, 256), F32),
             pltpu.VMEM((8, 256), F32),
-            pltpu.VMEM((8, 8, 256), F32),
-            dma((9,)), dma((9,)), dma((7,)), dma((7,)), dma((7,)), dma((7,)),
+            pltpu.VMEM((8, 256), F32),
+            pltpu.VMEM((8, 256), F32),
+            pltpu.VMEM((4, 8, 256), F32),
+            dma((8,)), dma((8,)), dma((7,)), dma((7,)), dma((5,)), dma((5,)),
         ],
         compiler_params=pltpu.CompilerParams(
-            collective_id=0, has_side_effects=True, vmem_limit_bytes=58 << 20),
+            collective_id=0, has_side_effects=True, vmem_limit_bytes=46 << 20),
         name="fused",
     )
 
 
 def body(samples, targets, counts, bucket_ids, sign_bits):
     rows = samples.shape[0]
+    operands = (samples, targets.reshape(rows // 128, 128), counts, bucket_ids, sign_bits)
     gram, zty = fused_call(rows)(
-        samples, targets.reshape(rows // 128, 128), counts, bucket_ids, sign_bits)
+        *[pltpu.with_memory_space_constraint(value, pltpu.HBM) for value in operands])
     return gram, zty.reshape(256)
 
 

time: 47.5 us -> 42.4 us (0.89)
  Pallas kernels: 44.5 us -> 40.4 us
  local copies, waits for them, and re-layouts: 2.24 us -> 1.27 us
    pallas_call x1, Pallas kernels: 44.5 us -> 40.4 us  [body(): fused_call(rows)]
    unnamed x4 -> x2, local copies, waits for them, and re-layouts: 2.24 us -> 1.27 us
where the time goes in v3:
time: 42.4 us; the launch traced here: 42.3 us
  Pallas kernels  40.4 us (95%)
  local copies, waits for them, and re-layouts  1.27 us (3%)
  between operations  0.64 us (2%)
    pallas_call x1, Pallas kernels, body(): fused_call(rows)  40.4 us
    unnamed x2, local copies, waits for them, and re-layouts  1.27 us

profile of v3, /device:TPU:1, one launch (start us, length us, event | category | flops | bytes accessed | tf_op | source)
XLA Modules:
  0.0 42.3 jit_solution(3058834068643151147)
XLA Ops:
  0.6 40.4 %fused.1 = (f32[256,256]{1,0:T(8,128)S(1)}, f32[1,256]{1,0:T(1,128)S(1)}) custom-call(bf16[768,256]{1,0:T(8,128)(2,1)} %x_hbm.1, bf16[6,128]{1,0:T(8,128)(2,1)} %bitcast.3, s32[16]{0:T(128)} %count_hbm.1, s32[3,256]{1,0:T(4,128)} %bid_hbm.1, s32[3,256]{1,0:T(4,128)} %sign_hbm.1), custom_call_target="tpu_custom_call" | custom-call | tf_op jit(solution)/shard_map/fused/pallas_call | solution.py:403
  41.0 0.7 %copy.9 = f32[256,256]{1,0:T(8,128)} copy(f32[256,256]{1,0:T(8,128)S(1)} %get-tuple-element.8) | data formatting | bytes 524288
  41.7 0.6 %copy.10 = f32[256]{0:T(256)} copy(f32[256]{0:T(256)S(1)} %bitcast.2) | data formatting | bytes 2048

commit v4 on v3

--- a/solution.py
+++ b/solution.py
@@ -33,23 +33,19 @@
     return lax.broadcasted_iota(I32, shape, dim)
 
 
-def setup(bid_ref, sign_ref, e_ref, step_ref, base_ref):
-    for k in range(3):
-        packed = bid_ref[k:k + 1, :] + SK * sign_ref[k:k + 1, :]
-        eye = iota((256, 256), 0) == iota((256, 256), 1)
-        column = jnp.sum(jnp.where(eye, packed.astype(F32), 0.0), axis=1, keepdims=True)
-        column = jnp.broadcast_to(column, (256, 128)).astype(I32)
-        b = column & (SK - 1)
-        s = (2 * (column >> 12) - 1).astype(F32)
-        step_ref[k, 0] = cos_turn(b, SK)
-        step_ref[k, 1] = -sin_turn(b, SK)
-        for half in range(2):
-            n = b * (iota((256, 128), 1) + 128 * half)
-            e_ref[k, half, 0] = s * cos_turn(n, 256)
-            e_ref[k, half, 1] = -s * sin_turn(n, 256)
-    n = iota((256, 256), 0) * iota((256, 256), 1)
-    base_ref[0] = cos_turn(n, 256)
-    base_ref[1] = sin_turn(n, 256)
+def dot(a, b):
+    return jnp.dot(a, b, preferred_element_type=F32)
+
+
+EVEN, ODD = (2, 4, 6, 8, 10, 12, 14), (1, 3, 5, 7, 9, 11, 13, 15)
+
+
+def column(k, bid_ref, sign_ref):
+    packed = bid_ref[k:k + 1, :] + SK * sign_ref[k:k + 1, :]
+    eye = iota((256, 256), 0) == iota((256, 256), 1)
+    both = jnp.sum(jnp.where(eye, packed.astype(F32), 0.0), axis=1, keepdims=True)
+    both = jnp.broadcast_to(both, (256, 128)).astype(I32)
+    return both & (SK - 1), (2 * (both >> 12) - 1).astype(F32)
 
 
 def put_split(t_ref, col, value):
@@ -58,63 +54,58 @@
     t_ref[256:512, col:col + 128] = (value - hi.astype(F32)).astype(BF)
 
 
-def table_first(e_ref, step_ref, ta, tb):
-    for k in range(3):
-        sr, si = step_ref[k, 0], step_ref[k, 1]
-        er, ei = e_ref[k, 0, 0], e_ref[k, 0, 1]
-        s2r, s2i = sr * sr - si * si, 2.0 * sr * si
-        s4r, s4i = s2r * s2r - s2i * s2i, 2.0 * s2r * s2i
-        s8r, s8i = s4r * s4r - s4i * s4i, 2.0 * s4r * s4i
-        lane = iota((256, 128), 1)
-        nyq = jnp.sum(jnp.where(lane == 0, e_ref[k, 1, 0], 0.0), axis=1, keepdims=True)
-        put_split(ta, 256 * k, er)
-        put_split(ta, 256 * k + 128, jnp.where(lane == 0, nyq, ei))
-        put_split(tb, 256 * k, er * s8r - ei * s8i)
-        put_split(tb, 256 * k + 128, er * s8i + ei * s8r)
-
-
-def table_next(half, e_ref, step_ref, t_ref):
-    for k in range(3):
-        sr, si = step_ref[k, 0], step_ref[k, 1]
-        er, ei = e_ref[k, half, 0], e_ref[k, half, 1]
-        nr, ni = er * sr - ei * si, er * si + ei * sr
-        e_ref[k, half, 0] = nr
-        e_ref[k, half, 1] = ni
-        put_split(t_ref, 256 * k, nr)
-        put_split(t_ref, 256 * k + 128, ni)
+def table_first(k, bid_ref, sign_ref, e_ref, step_ref, t_ref):
+    b, s = column(k, bid_ref, sign_ref)
+    lane = iota((256, 128), 1)
+    er, ei = s * cos_turn(b * lane, 128), -s * sin_turn(b * lane, 128)
+    e_ref[k, 0] = er
+    e_ref[k, 1] = ei
+    sr, si = cos_turn(b * lane, SK), -sin_turn(b * lane, SK)
+    step_ref[k, 0] = sr
+    step_ref[k, 1] = si
+    flip = (1 - 2 * (b & 1)).astype(F32)
+    hr, hi = flip * sr[:, 16:17], flip * si[:, 16:17]
+    low = lane < 64
+    put_split(t_ref, 256 * k, jnp.where(low, er, er * hr - ei * hi))
+    put_split(t_ref, 256 * k + 128, jnp.where(lane == 0, s * flip, jnp.where(low, ei, er * hi + ei * hr)))
+
+
+def table_next(k, g, e_ref, step_ref, t_ref):
+    sr, si = step_ref[k, 0, :, g:g + 1], step_ref[k, 1, :, g:g + 1]
+    er, ei = e_ref[k, 0], e_ref[k, 1]
+    put_split(t_ref, 256 * k, er * sr - ei * si)
+    put_split(t_ref, 256 * k + 128, er * si + ei * sr)
 
 
 def inverse_first(base_ref, w_ref):
-    c2 = iota((8, 256), 1)
-    r8, i8 = cos_turn(8 * c2, SK)[0:1], sin_turn(8 * c2, SK)[0:1]
-    c, s = base_ref[0, 0:128], base_ref[1, 0:128]
-    first = iota((128, 256), 0) == 0
-    gain = jnp.where(first, 1.0 / 64, 2.0 / 64)
-    alt = (1 - 2 * (iota((128, 256), 1) & 1)).astype(F32)
-    zero = jnp.zeros((128, 256), BF)
-    w_ref[0:128, 0:256] = (c * gain).astype(BF)
-    w_ref[0:128, 256:512] = zero
-    w_ref[128:256, 0:256] = jnp.where(first, alt * (1.0 / 64), s * (-2.0 / 64)).astype(BF)
-    w_ref[128:256, 256:512] = zero
-    w_ref[256:384, 0:256] = zero
-    w_ref[256:384, 256:512] = ((c * r8 - s * i8) * (2.0 / 64)).astype(BF)
-    w_ref[384:512, 0:256] = zero
-    w_ref[384:512, 256:512] = ((s * r8 + c * i8) * (-2.0 / 64)).astype(BF)
+    n = iota((128, 128), 0) * iota((128, 128), 1)
+    base_ref[0] = cos_turn(n, 128)
+    base_ref[1] = sin_turn(n, 128)
+    row = iota((128, 128), 0)
+    c2 = iota((128, 128), 1)
+    low = row < 64
+    f = jnp.where(low, 32 * row, 16 + 32 * (row - 64))
+    gain = jnp.where(row == 0, 1.0 / 64, 2.0 / 64)
+    wr = cos_turn(f * c2, SK) * gain
+    wi = sin_turn(f * c2, SK) * (-2.0 / 64)
+    wi = jnp.where(row == 0, (1 - 2 * (c2 & 1)).astype(F32) * (1.0 / 64), wi)
+    for at, w in ((0, wr), (128, wi)):
+        w_ref[at:at + 128, 0:128] = jnp.where(low, w, 0.0).astype(BF)
+        w_ref[at:at + 128, 128:256] = jnp.where(low, 0.0, w).astype(BF)
 
 
 def inverse_next(g, base_ref, w_ref):
-    c2 = iota((8, 256), 1)
+    c2 = iota((8, 128), 1)
     r, i = cos_turn(g * c2, SK)[0:1] * (2.0 / 64), sin_turn(g * c2, SK)[0:1] * (2.0 / 64)
-    for half in range(2):
-        c, s = base_ref[0, 128 * half:128 * half + 128], base_ref[1, 128 * half:128 * half + 128]
-        wr, wi = c * r - s * i, s * r + c * i
-        w_ref[256 * half:256 * half + 128, 0:256] = wr.astype(BF)
-        w_ref[256 * half:256 * half + 128, 256:512] = wi.astype(BF)
-        w_ref[256 * half + 128:256 * half + 256, 0:256] = (-wi).astype(BF)
-        w_ref[256 * half + 128:256 * half + 256, 256:512] = wr.astype(BF)
-
-
-def multiply(rows, first, spec_ref, cube_ref, p_ref, half):
+    c, s = base_ref[0], base_ref[1]
+    wr, wi = c * r - s * i, s * r + c * i
+    w_ref[0:128, 0:128] = wr.astype(BF)
+    w_ref[0:128, 128:256] = wi.astype(BF)
+    w_ref[128:256, 0:128] = (-wi).astype(BF)
+    w_ref[128:256, 128:256] = wr.astype(BF)
+
+
+def multiply(rows, first, spec_ref, cube_ref, p_ref):
     block = 16
     for n in range(rows // block):
         r = slice(block * n, block * n + block)
@@ -127,95 +118,141 @@
             lane = iota((block, 128), 1) == 0
             yr = jnp.where(lane, ar * br * cr, yr)
             yi = jnp.where(lane, ai * bi * ci, yi)
-        p_ref[r, 256 * half:256 * half + 128] = yr.astype(BF)
-        p_ref[r, 256 * half + 128:256 * half + 256] = yi.astype(BF)
-
-
-def combine(rows, y_ref, f_ref):
+        p_ref[r, 0:128] = yr.astype(BF)
+        p_ref[r, 128:256] = yi.astype(BF)
+
+
+def real_sixteen(y0, y8, re, im):
+    h, C, S = (jnp.float32(v) for v in (math.sqrt(0.5), math.cos(math.pi / 8), math.sin(math.pi / 8)))
+    a, b = y0 + y8, y0 - y8
+    r4, i4 = re(4), im(4)
+    ee = [a + r4, b - i4, a - r4, b + i4]
+    r2, i2, r6, i6 = re(2), im(2), re(6), im(6)
+    d, e = h * (r2 - r6), h * (i2 + i6)
+    eo = [r2 + r6, d - e, i6 - i2, -d - e]
+    even = [ee[q] + eo[q] for q in range(4)] + [ee[q] - eo[q] for q in range(4)]
+    r1, r7, i1, i7 = re(1), re(7), im(1), im(7)
+    r3, r5, i3, i5 = re(3), re(5), im(3), im(5)
+    p1, m1, q1, n1 = r1 + r7, r1 - r7, i1 - i7, i1 + i7
+    p3, m3, q3, n3 = r3 + r5, r3 - r5, i3 - i5, i3 + i5
+    dp, dq = h * (p1 - p3), h * (q1 + q3)
+    u1, v1 = m1 * C + m3 * S, n1 * S + n3 * C
+    u3, v3 = m1 * S - m3 * C, n1 * C - n3 * S
+    odd = [p1 + p3, u1 - v1, dp - dq, u3 - v3, q3 - q1, -u3 - v3, -dp - dq, -u1 - v1]
+    return [even[q] + odd[q] for q in range(8)] + [even[q] - odd[q] for q in range(8)]
+
+
+def combine_even(start, stop, y_ref):
+    for n in range(start, stop):
+        r = slice(8 * n, 8 * n + 8)
+        out = real_sixteen(y_ref[0, r, 0:128], y_ref[0, r, 128:256],
+                           lambda g: y_ref[g, r, 0:128], lambda g: y_ref[g, r, 128:256])
+        for q in range(16):
+            y_ref[q // 2, r, 128 * (q % 2):128 * (q % 2) + 128] = out[q]
+
+
+def combine_odd(rows, y_ref, f_ref):
     block = 16
+    cos = lambda n: jnp.float32(math.cos(math.pi * n / 16))
+    sin = lambda n: jnp.float32(math.sin(math.pi * n / 16))
     h, C, S = (jnp.float32(v) for v in (math.sqrt(0.5), math.cos(math.pi / 8), math.sin(math.pi / 8)))
 
-    def step(n, carry):
+    def put(r, q, value, f_ref):
+        lanes = slice(128 * (q % 2), 128 * (q % 2) + 128)
+        even = y_ref[q // 2, r, lanes]
+        f_ref[q // 2, r, lanes] = (even + value).astype(BF)
+        f_ref[8 + q // 2, r, lanes] = (even - value).astype(BF)
+
+    def parts(r, sign):
+        re = lambda g: y_ref[8 + g // 2, r, 0:128]
+        im = lambda g: y_ref[8 + g // 2, r, 128:256]
+        a = {g: re(g) + re(16 - g) if sign > 0 else re(g) - re(16 - g) for g in (1, 3, 5, 7)}
+        b = {g: im(g) - im(16 - g) if sign > 0 else im(g) + im(16 - g) for g in (1, 3, 5, 7)}
+        return a, b
+
+    def evens(n, carry):
         r = pl.ds(pl.multiple_of(n * block, block), block)
-        for half in range(2):
-            lo = slice(128 * half, 128 * half + 128)
-            hi = slice(256 + 128 * half, 256 + 128 * half + 128)
-            re = lambda g: y_ref[g, r, lo]
-            im = lambda g: y_ref[g, r, hi]
-            y0, y8 = re(0), im(0)
-            a, b = y0 + y8, y0 - y8
-            r4, i4 = re(4), im(4)
-            ee = [a + r4, b - i4, a - r4, b + i4]
-            r2, i2, r6, i6 = re(2), im(2), re(6), im(6)
-            d, e = h * (r2 - r6), h * (i2 + i6)
-            eo = [r2 + r6, d - e, i6 - i2, -d - e]
-            even = [ee[q] + eo[q] for q in range(4)] + [ee[q] - eo[q] for q in range(4)]
-            r1, r7, i1, i7 = re(1), re(7), im(1), im(7)
-            r3, r5, i3, i5 = re(3), re(5), im(3), im(5)
-            p1, m1, q1, n1 = r1 + r7, r1 - r7, i1 - i7, i1 + i7
-            p3, m3, q3, n3 = r3 + r5, r3 - r5, i3 - i5, i3 + i5
-            dp, dq = h * (p1 - p3), h * (q1 + q3)
-            u1, v1 = m1 * C + m3 * S, n1 * S + n3 * C
-            u3, v3 = m1 * S - m3 * C, n1 * C - n3 * S
-            odd = [p1 + p3, u1 - v1, dp - dq, u3 - v3, q3 - q1, -u3 - v3, -dp - dq, -u1 - v1]
-            for q in range(8):
-                f_ref[q, r, lo] = (even[q] + odd[q]).astype(BF)
-                f_ref[q + 8, r, lo] = (even[q] - odd[q]).astype(BF)
+        p, q = parts(r, 1)
+        p1, m1, q1, n1 = p[1] + p[7], p[1] - p[7], q[1] - q[7], q[1] + q[7]
+        p3, m3, q3, n3 = p[3] + p[5], p[3] - p[5], q[3] - q[5], q[3] + q[5]
+        put(r, 0, p1 + p3, f_ref)
+        put(r, 8, q3 - q1, f_ref)
+        dp, dq = h * (p1 - p3), h * (q1 + q3)
+        put(r, 4, dp - dq, f_ref)
+        put(r, 12, -dp - dq, f_ref)
+        u1, v1 = m1 * C + m3 * S, n1 * S + n3 * C
+        put(r, 2, u1 - v1, f_ref)
+        put(r, 14, -u1 - v1, f_ref)
+        u3, v3 = m1 * S - m3 * C, n1 * C - n3 * S
+        put(r, 6, u3 - v3, f_ref)
+        put(r, 10, -u3 - v3, f_ref)
         return carry
 
-    lax.fori_loop(0, rows // block, step, 0)
-
-
-def dot(a, b):
-    return jnp.dot(a, b, preferred_element_type=F32)
-
-
-def features(rows, x2, cube, e_ref, step_ref, base_ref, ta, tb, w_ref, sa, sb, p_ref, y_ref, f_ref):
-    table_first(e_ref, step_ref, ta, tb)
-    sa[...] = dot(x2[...], ta[...])
-    inverse_first(base_ref, w_ref)
-    sb[...] = dot(x2[...], tb[...])
-    multiply(rows, True, sa, cube, p_ref, 0)
-    table_next(0, e_ref, step_ref, ta)
-
-    def step(g, carry):
-        sa[...] = dot(x2[...], ta[...])
-        multiply(rows, False, sb, cube, p_ref, 1)
-        table_next(1, e_ref, step_ref, tb)
-        y_ref[g - 1] = dot(p_ref[...], w_ref[...])
-        sb[...] = dot(x2[...], tb[...])
-        multiply(rows, False, sa, cube, p_ref, 0)
-        table_next(0, e_ref, step_ref, ta)
-        inverse_next(g, base_ref, w_ref)
+    def odds(n, carry):
+        r = pl.ds(pl.multiple_of(n * block, block), block)
+        m, w = parts(r, -1)
+        for c in (1, 3, 5, 7):
+            u = m[1] * cos(c) + m[3] * cos(3 * c) + m[5] * cos(5 * c) + m[7] * cos(7 * c)
+            v = w[1] * sin(c) + w[3] * sin(3 * c) + w[5] * sin(5 * c) + w[7] * sin(7 * c)
+            put(r, c, u - v, f_ref)
+            put(r, 16 - c, -u - v, f_ref)
         return carry
 
-    lax.fori_loop(1, 8, step, 0)
-    multiply(rows, False, sb, cube, p_ref, 1)
-    y_ref[7] = dot(p_ref[...], w_ref[...])
-    combine(rows, y_ref, f_ref)
+    lax.fori_loop(0, rows // block, evens, 0, unroll=2)
+    lax.fori_loop(0, rows // block, odds, 0, unroll=2)
+
+
+def sketch(rows, bid_ref, sign_ref, x2, cube, e_ref, step_ref, base_ref, ta, tb, wa, wb, sa, sb, pa, pb,
+           y_ref, f_ref):
+    inverse_first(base_ref, wa)
+    for k in range(3):
+        table_first(k, bid_ref, sign_ref, e_ref, step_ref, ta)
+        lanes = slice(256 * k, 256 * k + 256)
+        sa[:, lanes] = dot(x2[...], ta[:, lanes])
+    groups = EVEN + ODD
+    slots = [0] + [g // 2 + 8 * (g % 2) for g in groups]
+    for k in range(3):
+        table_next(k, groups[0], e_ref, step_ref, tb)
+    inverse_next(groups[0], base_ref, wb)
+    bufs = ((ta, wa, sa, pa), (tb, wb, sb, pb))
+    blocks = rows // 8
+    for n in range(1, 16):
+        t, w, s, p = bufs[n % 2]
+        t_old, w_old, s_old, p_old = bufs[(n + 1) % 2]
+        s[...] = dot(x2[...], t[...])
+        multiply(rows, n == 1, s_old, cube, p_old)
+        if n < 15:
+            g = groups[n]
+            for k in range(3):
+                table_next(k, g, e_ref, step_ref, t_old)
+        y_ref[slots[n - 1]] = dot(p_old[...], w_old[...])
+        if n < 15:
+            inverse_next(g, base_ref, w_old)
+        if n >= 9 and n < 15:
+            combine_even(blocks * (n - 9) // 6, blocks * (n - 8) // 6, y_ref)
+    multiply(rows, False, sb, cube, pb)
+    y_ref[slots[15]] = dot(pb[...], wb[...])
+    combine_odd(rows, y_ref, f_ref)
 
 
 def scratch(rows):
     return [
         pltpu.VMEM((rows, 512), BF),
         pltpu.VMEM((rows, 128), F32),
-        pltpu.VMEM((3, 2, 2, 256, 128), F32),
         pltpu.VMEM((3, 2, 256, 128), F32),
-        pltpu.VMEM((2, 256, 256), F32),
+        pltpu.VMEM((3, 2, 256, 128), F32),
+        pltpu.VMEM((2, 128, 128), F32),
         pltpu.VMEM((512, 768), BF),
         pltpu.VMEM((512, 768), BF),
-        pltpu.VMEM((512, 512), BF),
+        pltpu.VMEM((256, 256), BF),
+        pltpu.VMEM((256, 256), BF),
         pltpu.VMEM((rows, 768), F32),
         pltpu.VMEM((rows, 768), F32),
-        pltpu.VMEM((rows, 512), BF),
-        pltpu.VMEM((8, rows, 512), F32),
+        pltpu.VMEM((rows, 256), BF),
+        pltpu.VMEM((rows, 256), BF),
+        pltpu.VMEM((16, rows, 256), F32),
         pltpu.VMEM((16, rows, 256), BF),
     ]
-
-
-def sketch(rows, bid_ref, sign_ref, x2, cube, e_ref, step_ref, base_ref, ta, tb, w_ref, sa, sb, p_ref, y_ref, f_ref):
-    setup(bid_ref, sign_ref, e_ref, step_ref, base_ref)
-    features(rows, x2, cube, e_ref, step_ref, base_ref, ta, tb, w_ref, sa, sb, p_ref, y_ref, f_ref)
 
 
 MESH = pl.DeviceIdType.MESH

time: 42.4 us -> 40.5 us (0.955)
  Pallas kernels: 40.4 us -> 38.5 us
    pallas_call x1, Pallas kernels: 40.4 us -> 38.5 us  [body(): fused_call(rows)]
where the time goes in v4:
time: 40.5 us; the launch traced here: 40.4 us
  Pallas kernels  38.5 us (95%)
  local copies, waits for them, and re-layouts  1.27 us (3%)
  between operations  0.64 us (2%)
    pallas_call x1, Pallas kernels, body(): fused_call(rows)  38.5 us
    unnamed x2, local copies, waits for them, and re-layouts  1.27 us

profile of v4, /device:TPU:1, one launch (start us, length us, event | category | flops | bytes accessed | tf_op | source)
XLA Modules:
  0.0 40.4 jit_solution(15873881919126968564)
XLA Ops:
  0.6 38.5 %fused.1 = (f32[256,256]{1,0:T(8,128)S(1)}, f32[1,256]{1,0:T(1,128)S(1)}) custom-call(bf16[768,256]{1,0:T(8,128)(2,1)} %x_hbm.1, bf16[6,128]{1,0:T(8,128)(2,1)} %bitcast.3, s32[16]{0:T(128)} %count_hbm.1, s32[3,256]{1,0:T(4,128)} %bid_hbm.1, s32[3,256]{1,0:T(4,128)} %sign_hbm.1), custom_call_target="tpu_custom_call" | custom-call | tf_op jit(solution)/shard_map/fused/pallas_call | solution.py:440
  39.1 0.7 %copy.9 = f32[256,256]{1,0:T(8,128)} copy(f32[256,256]{1,0:T(8,128)S(1)} %get-tuple-element.8) | data formatting | bytes 524288
  39.8 0.6 %copy.10 = f32[256]{0:T(256)} copy(f32[256]{0:T(256)S(1)} %bitcast.2) | data formatting | bytes 2048
